TPU v7x, 32 devices: a whole 2x2x4 slice. The times are simulated.
32 devices in a mesh: rep: 2 (over core), space: 16 (over z, y, x).
Axes of the slice: x: 2, y: 2, z: 4, core: 2. Of those that a mesh axis runs over, the one named last changes fastest.
Arguments:
- particles: float32 [6, 2, 8192, 128], P(None, 'rep', 'space'), may hold values from -6 to 6
- pair_order: int32 [2, 8192, 128], P('rep', 'space'), may hold values from 0 to 127, each once within a row
- accepted: int32 [2, 8192, 64], P('rep', 'space'), may hold values 0 or 1
- direction: int32 [2, 8192, 64], P('rep', 'space'), may hold values from 0 to 255
- destination: int32 [2, 8192], P('rep', 'space'), may hold values from 0 to 15, as said below
- live_count: int32 [2, 16], P('rep', 'space'), may hold values from 256 to 512, as said below
- cell_index: int32 [2, 8192], P('rep', 'space'), may hold values from 0 to 255
Outputs:
- moved: float32 [6, 2, 12288, 128], P(None, 'rep', 'space')
- samples: float32 [4, 16, 256], P(None, 'space', 'rep')
Inputs may be any that keep to these rules, and one draw needn't show every extreme that they name: Every block's destination is its own slab or one of the two beside it, slab 0 and slab 16 - 1 being beside each other; only live blocks leave; one slab of one replica sends at most 128 blocks to each of its two neighbours, and in every replica some slab sends exactly 128 to its upper and some slab exactly 128 to its lower neighbour. `live_count`: the count of live blocks of each slab of each replica; slab 0 of replica 0 is full.
All inputs are finite; a program needn't handle non-finite values. No bound on the sum of `accepted` on one device may be relied on, other than what follows from the above.
Results may differ from a plain program's by a relative error of at most 0.0003.
Values sent between devices are 32-bit elements; how exact they have to be, the bound alone decides.
A program may use at most 64 MiB of HBM per device.

v0:
```python
import jax
import jax.numpy as jnp
from jax import lax
from jax.sharding import PartitionSpec as P

PART = 128
PAIRS = 64
NDIR = 256
CAP = 512
MOVE = 128
CELLS = 256


time_step = 0.25
golden_turn = 2.399963229728653
group_size = 16


def from_behind(value, axis, steps):
    count = lax.axis_size(axis)
    pairs = [(source, (source + steps) % count) for source in range(count)]
    return lax.ppermute(value, axis, pairs)


def directions(index):
    turns = index.astype(jnp.float32)
    height = 1.0 - (2.0 * turns + 1.0) / NDIR
    radius = jnp.sqrt(1.0 - height * height)
    angle = turns * golden_turn
    return jnp.stack([radius * jnp.cos(angle), radius * jnp.sin(angle), height])


def collide_group(inputs):
    velocity, order, flags, turns = inputs
    lanes = jnp.arange(PART, dtype=jnp.int32)
    onehot = (order[:, :, None] == lanes[None, None, :]).astype(jnp.float32)
    permuted = jnp.einsum("kbp,bqp->kbq", velocity, onehot, precision=lax.Precision.HIGHEST)
    first = permuted[:, :, :PAIRS]
    second = permuted[:, :, PAIRS:]
    center = 0.5 * (first + second)
    relative = first - second
    speed = jnp.sqrt(jnp.sum(relative * relative, axis=0))
    unit = directions(turns)
    taken = (flags == 1)[None]
    first_out = jnp.where(taken, center + 0.5 * speed * unit, first)
    second_out = jnp.where(taken, center - 0.5 * speed * unit, second)
    combined = jnp.concatenate([first_out, second_out], axis=2)
    return jnp.einsum("kbq,bqp->kbp", combined, onehot, precision=lax.Precision.HIGHEST)


def collide(velocity, orders, flags, turns):
    count = velocity.shape[1]
    groups = count // group_size
    grouped = jnp.moveaxis(velocity.reshape(3, groups, group_size, PART), 1, 0)
    result = lax.map(
        collide_group,
        (
            grouped,
            orders.reshape(groups, group_size, PART),
            flags.reshape(groups, group_size, PAIRS),
            turns.reshape(groups, group_size, PAIRS),
        ),
    )
    return jnp.moveaxis(result, 0, 1).reshape(3, count, PART)


def advance(current, orders, flags, turns):
    velocity = collide(current[3:], orders, flags, turns)
    position = current[:3] + time_step * velocity
    return (position, velocity)


def moments(velocity, living):
    sums = jnp.stack(
        [
            jnp.sum(velocity[0], axis=1),
            jnp.sum(velocity[1], axis=1),
            jnp.sum(velocity[2], axis=1),
            jnp.sum(jnp.sum(velocity * velocity, axis=0), axis=1),
        ]
    )
    return jnp.where(living[None], sums, 0.0)


def mover_slots(moving):
    ranking = jnp.cumsum(moving.astype(jnp.int32)) - 1
    slots = jnp.arange(MOVE, dtype=jnp.int32)
    matches = moving[None, :] & (ranking[None, :] == slots[:, None])
    sources = jnp.arange(moving.shape[0], dtype=jnp.int32)
    chosen = jnp.sum(jnp.where(matches, sources[None, :], 0), axis=1)
    is_valid = jnp.any(matches, axis=1)
    return (chosen, is_valid)


def per_device(particles, pair_order, accepted, direction, destination, live_count, cell_index):
    current = particles[:, 0]
    orders = pair_order[0]
    flags = accepted[0]
    turns = direction[0]
    my_slab = lax.axis_index("space")
    slab_total = lax.axis_size("space")
    upper_slab = (my_slab + 1) % slab_total
    lower_slab = (my_slab + slab_total - 1) % slab_total
    slot_index = jnp.arange(CAP, dtype=jnp.int32)
    living = slot_index < live_count[0, 0]
    targets = destination[0]
    to_upper = living & (targets == upper_slab)
    to_lower = living & (targets == lower_slab)
    staying = living & (targets == my_slab)
    upper_ids, upper_valid = mover_slots(to_upper)
    lower_ids, lower_valid = mover_slots(to_lower)
    position, velocity = advance(current, orders, flags, turns)
    updated = jnp.concatenate([position, velocity], axis=0)
    send_upper = jnp.where(upper_valid[None, :, None], jnp.take(updated, upper_ids, axis=1), 0.0)
    send_lower = jnp.where(lower_valid[None, :, None], jnp.take(updated, lower_ids, axis=1), 0.0)
    from_lower = from_behind(send_upper, "space", 1)
    from_upper = from_behind(send_lower, "space", -1)
    term = moments(velocity, living)
    cell_ids = jnp.arange(CELLS, dtype=jnp.int32)
    onehot = (cell_index[0][None, :] == cell_ids[:, None]).astype(jnp.float32)
    cell_terms = jnp.dot(term, onehot.T, precision=lax.Precision.HIGHEST)
    summed = lax.psum_scatter(cell_terms, "rep", scatter_dimension=1, tiled=True)
    samples = (summed / (PART * lax.axis_size("rep")))[:, None, :]
    keep = staying[None, :, None]
    moved = jnp.concatenate(
        [
            from_lower,
            jnp.where(keep, jnp.concatenate([position, velocity], axis=0), 0.0),
            from_upper,
        ],
        axis=1,
    )
    return (moved[:, None], samples)


def solution(mesh):
    return jax.shard_map(
        per_device,
        mesh=mesh,
        in_specs=(
            P(None, "rep", "space", None),
            P("rep", "space", None),
            P("rep", "space", None),
            P("rep", "space", None),
            P("rep", "space"),
            P("rep", "space"),
            P("rep", "space"),
        ),
        out_specs=(P(None, "rep", "space", None), P(None, "space", "rep")),
        check_vma=False,
    )
```

profile of v0, /device:TPU:0, one launch (start us, length us, event | category | flops | bytes accessed | tf_op | source)
XLA Modules:
  0.0 152.1 jit_solution(619784694886374812)
XLA Ops:
  9.5 1.0 copy.38
  10.6 1.0 copy.40
  11.6 1.5 fusion.28
  13.6 89.0 %while.10 = (s32[]{:T(128)}, f32[32,3,16,128]{3,1,2,0:T(4,128)S(1)}, s32[32,16,128]{2,1,0:T(8,128)}, s32[32,16,64]{2,1,0:T(8,128)S(1)}, f32[32,3,16,128]{3,1,2,0...) while((s32[]{:T(128)}, f32[32,3,16,128]{3,1,2,0:T(4,128)S(1)}, s32[32,16,128]{2,1,0:T(8,128)}, ...), condition=%wide.region_5.6_spmd, body=%wide.region_3.5_spmd.sunk | while | flops 19452928 | bytes 370793 | solution.py:55
  14.4 1.0 fusion.36
  17.2 1.0 fusion.36
  20.0 1.0 fusion.36
  22.8 1.0 fusion.36
  25.6 1.0 fusion.36
  28.3 1.0 fusion.36
  31.1 1.0 fusion.36
  33.9 1.0 fusion.36
  36.7 1.0 fusion.36
  39.5 1.0 fusion.36
  42.2 1.0 fusion.36
  45.0 1.0 fusion.36
  47.8 1.0 fusion.36
  50.6 1.0 fusion.36
  53.4 1.0 fusion.36
  56.2 1.0 fusion.36
  58.9 1.0 fusion.36
  61.7 1.0 fusion.36
  64.5 1.0 fusion.36
  67.3 1.0 fusion.36
  70.1 1.0 fusion.36
  72.8 1.0 fusion.36
  75.6 1.0 fusion.36
  78.4 1.0 fusion.36
  81.2 1.0 fusion.36
  84.0 1.0 fusion.36
  86.8 1.0 fusion.36
  89.5 1.0 fusion.36
  92.3 1.0 fusion.36
  95.1 1.0 fusion.36
  97.9 1.0 fusion.36
  100.7 1.0 fusion.36
  103.4 2.9 %broadcast_select_fusion = (f32[6,512,128]{2,0,1:T(8,128)S(1)}, f32[6,512,128]{2,0,1:T(8,128)}) fusion(pred[512]{0:T(512)(128)(4,1)S(1)} %fusion.27, f32[3,512,128]{2,0,1:T(4,128)S(1)} %bitcast.74, f32[3,512,128]{2,0,1:T(4,128)S(1)} %fusion.9), kind=kLoop, calls=%fused_computation.34 | loop fusion | flops 786432 | bytes 4719104 | tf_op jit(solution)/shard_map/jit(_where)/select_n | solution.py:128
  106.3 3.0 %gather_fusion.1 = f32[128,6,128]{2,1,0:T(8,128)} fusion(f32[6,512,128]{2,0,1:T(8,128)} %get-tuple-element.90, s32[1024]{0:T(1024)S(1)} %pad_clamp_fusion), kind=kCustom, calls=%fused_computation.1.clone | custom fusion | bytes 786944 | tf_op jit(solution)/shard_map/jit(_take)/gather | solution.py:115
  109.4 2.2 %bitcast_select_fusion = f32[6,128,128]{2,0,1:T(8,128)} fusion(f32[128,6,128]{2,1,0:T(8,128)} %gather_fusion.1, pred[128]{0:T(512)(128)(4,1)S(1)} %compare_and_fusion, pred[128]{0:T(512)(128)(4,1)S(1)} %fusion.14), kind=kLoop, calls=%fused_computation.35 | loop fusion | flops 196608 | bytes 786688 | tf_op jit(solution)/shard_map/jit(_where)/select_n | solution.py:115
  111.5 7.0 %collective-permute-start.1 = (f32[6,128,128]{2,0,1:T(8,128)}, f32[6,128,128]{2,0,1:T(8,128)}, u32[]{:S(2)}, u32[]{:S(2)}) collective-permute-start(f32[6,128,128]{2,0,1:T(8,128)} %bitcast_select_fusion), channel_id=1, source_target_pairs={{0,15},{1,0},{2,1},{3,2},{4,3},{5,4},{6,5},{7,6},{8,7},{9,8},{10,9... | collective-permute-start | bytes 1179656 | tf_op jit(solution)/shard_map/ppermute | solution.py:22
  119.4 3.0 %gather_fusion = f32[128,6,128]{2,1,0:T(8,128)} fusion(f32[6,512,128]{2,0,1:T(8,128)} %get-tuple-element.90, s32[1024]{0:T(1024)S(1)} %pad_clamp_fusion.1), kind=kCustom, calls=%fused_computation.clone | custom fusion | bytes 786944 | tf_op jit(solution)/shard_map/jit(_take)/gather | solution.py:114
  122.5 2.2 %bitcast_select_fusion.1 = f32[6,128,128]{2,0,1:T(8,128)} fusion(f32[128,6,128]{2,1,0:T(8,128)} %gather_fusion, pred[128]{0:T(512)(128)(4,1)S(1)} %compare_and_fusion.1, pred[128]{0:T(512)(128)(4,1)S(1)} %fusion.12), kind=kLoop, calls=%fused_computation.36 | loop fusion | flops 196608 | bytes 786688 | tf_op jit(solution)/shard_map/jit(_where)/select_n | solution.py:114
  125.7 2.9 %slice_reduce_fusion.2 = (f32[32,16]{1,0:T(8,128)S(1)}, f32[32,16]{1,0:T(8,128)S(1)}, f32[32,16]{1,0:T(8,128)S(1)}) fusion(f32[3,32,16,128]{3,0,2,1:T(4,128)S(1)} %bitcast.75), kind=kLoop, calls=%fused_computation.40 | loop fusion | flops 195072 | bytes 792576 | tf_op jit(solution)/shard_map/reduce_sum | solution.py:76
  128.8 1.0 convolution_bitcast_fusion.1
  129.9 9.1 %reduce-scatter.4.cloned.1.call-done = f32[128,4]{1,0:T(8,128)} async-done(((f32[256,4]{1,0:T(8,128)}), f32[128,4]{1,0:T(8,128)}) %reduce-scatter.4.cloned.1.call-update) | async-done | bytes 2064
  140.5 1.4 collective-permute-done
  141.9 1.5 maximum_bitcast_fusion
  143.5 1.8 %copy.41 = f32[6,1,768,128]{3,2,1,0:T(8,128)} copy(f32[6,1,768,128]{3,0,2,1:T(8,128)S(1)} %maximum_bitcast_fusion) | data formatting | bytes 4718592
  (329 shorter events, 63.3 us)
Async XLA Ops:
  7.2 131.8 %reduce-scatter.4.cloned.1.call-start = ((), (), s32[]{:S(2)}) async-start(), calls=%async_computation.1 | async-start | bytes 196608
  111.5 17.3 %copy-start = (s32[1,512]{1,0:T(1,128)S(1)}, s32[1,512]{1,0:T(1,128)}, u32[]{:S(2)}) copy-start(s32[1,512]{1,0:T(1,128)} %param.17) | copy-start | bytes 6148
  111.5 29.0 %collective-permute-start.1 = (f32[6,128,128]{2,0,1:T(8,128)}, f32[6,128,128]{2,0,1:T(8,128)}, u32[]{:S(2)}, u32[]{:S(2)}) collective-permute-start(f32[6,128,128]{2,0,1:T(8,128)} %bitcast_select_fusion), channel_id=1, source_target_pairs={{0,15},{1,0},{2,1},{3,2},{4,3},{5,4},{6,5},{7,6},{8,7},{9,8},{10,9... | collective-permute-start | bytes 1179656 | tf_op jit(solution)/shard_map/ppermute | solution.py:22
  124.6 17.3 %collective-permute-start = (f32[6,128,128]{2,0,1:T(8,128)}, f32[6,128,128]{2,0,1:T(8,128)}, u32[]{:S(2)}, u32[]{:S(2)}) collective-permute-start(f32[6,128,128]{2,0,1:T(8,128)} %bitcast_select_fusion.1), channel_id=1, source_target_pairs={{0,1},{1,2},{2,3},{3,4},{4,5},{5,6},{6,7},{7,8},{8,9},{9,10},{10,1... | collective-permute-start | bytes 1179656 | tf_op jit(solution)/shard_map/ppermute | solution.py:22
Sparse Core Ops, SparseCore 0:
  130.0 8.9 reduce-scatter.3
where the time goes:
time: 154 us; the launch traced here: 152 us
  matrix products  56 us (36%)
  local copies, waits for them, and re-layouts  36.3 us (24%)
  other arithmetic  26.5 us (17%)
  between operations  14.8 us (10%)
  waiting for transfers between devices  10.6 us (7%)
  starting transfers between devices  7 us (5%)
    dot_general x32, matrix products, collide_group(): jnp.einsum('kbp,bqp->kbq', velocity, onehot, precision=lax.Precision.HIGH...  31.5 us
    dot_general x32, matrix products, collide_group(): jnp.einsum('kbq,bqp->kbp', combined, onehot, precision=lax.Precision.HIGH...  23.5 us
    eq x32, local copies, waits for them, and re-layouts, collide_group(): onehot = (order[:, :, None] == lanes[None, None, :]).astype(jnp.float32)  22.5 us
    unnamed x2, waiting for transfers between devices  9.14 us
    ppermute x2, starting transfers between devices, from_behind(): return lax.ppermute(value, axis, pairs)  6.96 us
    unnamed x6, local copies, waits for them, and re-layouts  4.79 us
  transfers between devices with their start and end apart: 3, of which 2 were waited for; matrix products, arithmetic and copies ran while one was open for 8% of the time, Pallas kernels for 0%

commit v1 on v0

v1 whole, which is shorter than its diff:
```python
import functools

import jax
import jax.numpy as jnp
from jax import lax
from jax.experimental import pallas as pl
from jax.experimental.pallas import tpu as pltpu
from jax.sharding import PartitionSpec as P

NDIR = 256
MOVE = 128
CELLS = 256
TIME_STEP = 0.25
GOLDEN_TURN = 2.399963229728653
ROWS = 32


def take_lanes(values, index):
    return jnp.take_along_axis(values, index, axis=1, mode="promise_in_bounds")


def split3(value):
    high = value.astype(jnp.bfloat16)
    rest = value - high.astype(jnp.float32)
    middle = rest.astype(jnp.bfloat16)
    low = (rest - middle.astype(jnp.float32)).astype(jnp.bfloat16)
    return high, middle, low


def dot(left, right):
    return jnp.dot(left, right, preferred_element_type=jnp.float32)


def dot_nt(left, right):
    return lax.dot_general(left, right, (((1,), (1,)), ((), ())), preferred_element_type=jnp.float32)


def inverse_order(order, lane):
    part = order.shape[1]
    key = (order * part + lane).astype(jnp.float32)
    size = 2
    while size <= part:
        stride = size // 2
        while stride >= 1:
            partner = take_lanes(key, lane ^ stride)
            keep_low = ((lane & stride) == 0) == ((lane & size) == 0)
            key = jnp.where(keep_low, jnp.minimum(key, partner), jnp.maximum(key, partner))
            stride //= 2
        size *= 2
    return key.astype(jnp.int32) - lane * part


def main_kernel(slabs, part_ref, order_ref, flag_ref, turn_ref, dest_ref, live_ref, cell_ref,
                moved_ref, up_ref, down_ref, cells_ref, table, packed_t, keep_t, parts, square):
    step = pl.program_id(0)
    steps = pl.num_programs(0)
    chunk, part = order_ref.shape
    pairs = part // 2
    cap = dest_ref.shape[1]
    my_slab = lax.axis_index("space")
    upper_slab = lax.rem(my_slab + 1, slabs)
    lower_slab = lax.rem(my_slab + slabs - 1, slabs)

    @pl.when(step == 0)
    def _():
        for half in range(2):
            turns = (lax.broadcasted_iota(jnp.int32, (8, part), 1) + half * part).astype(jnp.float32)
            height = 1.0 - (2.0 * turns + 1.0) / NDIR
            radius = jnp.sqrt(1.0 - height * height)
            angle = turns * GOLDEN_TURN
            table[half] = radius * jnp.cos(angle)
            table[half + 2] = radius * jnp.sin(angle)

    pair_code = turn_ref[...] + NDIR * flag_ref[...]
    packed_t[...] = jnp.transpose(jnp.concatenate([pair_code, pair_code], axis=0))
    start = pl.multiple_of(step * chunk, chunk)
    slots = lax.broadcasted_iota(jnp.int32, (1, chunk), 1) + step * chunk
    staying = (dest_ref[:, pl.ds(start, chunk)] == my_slab) & (slots < live_ref[0, 0])
    stay_rows = jnp.broadcast_to(jnp.where(staying, 1.0, 0.0), (part, chunk))
    keep_t[...] = jnp.transpose(stay_rows)

    def rows_step(i, carry):
        row = pl.multiple_of(i * ROWS, ROWS)
        here = pl.ds(row, ROWS)
        lane = lax.broadcasted_iota(jnp.int32, (ROWS, part), 1)
        order = order_ref[here, :]
        inverse = inverse_order(order, lane)
        partner = take_lanes(order, inverse ^ pairs)
        code = take_lanes(packed_t[here, :], inverse & (pairs - 1))
        taken = code >= NDIR
        turn = code & (NDIR - 1)
        low_index = turn & (part - 1)
        is_high = turn >= part
        wide = (ROWS, part)
        tables = [jnp.broadcast_to(table[k, 0:1, :], wide) for k in range(4)]
        unit_x = jnp.where(is_high, take_lanes(tables[1], low_index), take_lanes(tables[0], low_index))
        unit_y = jnp.where(is_high, take_lanes(tables[3], low_index), take_lanes(tables[2], low_index))
        unit_z = 1.0 - (2.0 * turn.astype(jnp.float32) + 1.0) / NDIR
        old = [part_ref[3 + k, here, :] for k in range(3)]
        other = [take_lanes(v, partner) for v in old]
        relative = [a - b for a, b in zip(old, other)]
        speed = jnp.sqrt(relative[0] * relative[0] + relative[1] * relative[1] + relative[2] * relative[2])
        half_speed = jnp.where(inverse < pairs, 0.5, -0.5) * speed
        new = [
            jnp.where(taken, 0.5 * (a + b) + half_speed * u, a)
            for a, b, u in zip(old, other, (unit_x, unit_y, unit_z))
        ]
        keep = keep_t[here, :] > 0.0
        block = pl.ds(pl.multiple_of(step * chunk + row, ROWS), ROWS)
        square[block, :] = new[0] * new[0] + new[1] * new[1] + new[2] * new[2]
        moving = [part_ref[k, here, :] + TIME_STEP * new[k] for k in range(3)]
        for k, value in enumerate(moving + new):
            moved_ref[k, here, :] = jnp.where(keep, value, 0.0)
            for j, piece in enumerate(split3(value)):
                parts[j, block, pl.ds(k * part, part)] = piece
        return carry

    lax.fori_loop(0, chunk // ROWS, rows_step, 0)

    @pl.when(step == steps - 1)
    def _():
        all_slots = lax.broadcasted_iota(jnp.int32, (1, cap), 1)
        living = all_slots < live_ref[0, 0]
        to_upper = living & (dest_ref[...] == upper_slab)
        to_lower = living & (dest_ref[...] == lower_slab)
        eight = lax.broadcasted_iota(jnp.int32, (8, cap), 0)
        both = jnp.where(eight == 0, jnp.where(to_upper, 1.0, 0.0), jnp.where(to_lower, 1.0, 0.0))
        triangle = (
            lax.broadcasted_iota(jnp.int32, (cap, cap), 0) <= lax.broadcasted_iota(jnp.int32, (cap, cap), 1)
        )
        ranking = dot(both.astype(jnp.bfloat16), jnp.where(triangle, 1.0, 0.0).astype(jnp.bfloat16))
        ranking = ranking.astype(jnp.int32) - 1
        up_slot = jnp.where(to_upper, ranking[0:1, :], -1)
        down_slot = jnp.where(to_lower, ranking[1:2, :], -1)
        slot = lax.broadcasted_iota(jnp.int32, (MOVE, cap), 0)
        chosen = jnp.concatenate(
            [jnp.where(slot == up_slot, 1.0, 0.0), jnp.where(slot == down_slot, 1.0, 0.0)], axis=0
        ).astype(jnp.bfloat16)
        for k in range(0, 6, 2):
            here = pl.ds(k * part, 2 * part)
            sent = dot(chosen, parts[0, :, here]) + dot(chosen, parts[1, :, here]) + dot(chosen, parts[2, :, here])
            for j in range(2):
                up_ref[k + j] = sent[:MOVE, j * part:(j + 1) * part]
                down_ref[k + j] = sent[MOVE:, j * part:(j + 1) * part]

        ones = jnp.ones((8, part), jnp.bfloat16)
        terms = []
        for k in range(3):
            here = pl.ds((3 + k) * part, part)
            terms.append(dot_nt(ones, parts[0, :, here]) + dot_nt(ones, parts[1, :, here]) + dot_nt(ones, parts[2, :, here]))
        pieces = split3(square[...])
        terms.append(dot_nt(ones, pieces[0]) + dot_nt(ones, pieces[1]) + dot_nt(ones, pieces[2]))
        term = jnp.where(eight == 0, terms[0], jnp.where(eight == 1, terms[1], jnp.where(eight == 2, terms[2], terms[3])))
        term = jnp.where(living, term, 0.0)
        cells = lax.broadcasted_iota(jnp.int32, (CELLS, cap), 0)
        in_cell = jnp.where(cells == cell_ref[...], 1.0, 0.0).astype(jnp.bfloat16)
        high, middle, low = split3(term)
        total = dot_nt(high, in_cell) + dot_nt(middle, in_cell) + dot_nt(low, in_cell)
        cells_ref[...] = total[0:4, :]


def from_behind(value, axis, steps):
    count = lax.axis_size(axis)
    pairs = [(source, (source + steps) % count) for source in range(count)]
    return lax.ppermute(value, axis, pairs)


def per_device(particles, pair_order, accepted, direction, destination, live_count, cell_index):
    six, _, cap, part = particles.shape
    pairs = accepted.shape[2]
    chunk = MOVE
    steps = cap // chunk
    slabs = lax.axis_size("space")
    reps = lax.axis_size("rep")
    f32 = jnp.float32
    out_cap = cap + 2 * MOVE
    moved, send_upper, send_lower, cell_terms = pl.pallas_call(
        functools.partial(main_kernel, slabs),
        grid=(steps,),
        in_specs=[
            pl.BlockSpec((six, chunk, part), lambda i: (0, i, 0)),
            pl.BlockSpec((chunk, part), lambda i: (i, 0)),
            pl.BlockSpec((pairs, chunk), lambda i: (0, i)),
            pl.BlockSpec((pairs, chunk), lambda i: (0, i)),
            pl.BlockSpec((1, cap), lambda i: (0, 0)),
            pl.BlockSpec(memory_space=pltpu.SMEM),
            pl.BlockSpec((1, cap), lambda i: (0, 0)),
        ],
        out_specs=[
            pl.BlockSpec((six, chunk, part), lambda i: (0, i + 1, 0)),
            pl.BlockSpec((six, MOVE, part), lambda i: (0, 0, 0)),
            pl.BlockSpec((six, MOVE, part), lambda i: (0, 0, 0)),
            pl.BlockSpec((4, CELLS), lambda i: (0, 0)),
        ],
        out_shape=[
            jax.ShapeDtypeStruct((six, out_cap, part), f32),
            jax.ShapeDtypeStruct((six, MOVE, part), f32),
            jax.ShapeDtypeStruct((six, MOVE, part), f32),
            jax.ShapeDtypeStruct((4, CELLS), f32),
        ],
        scratch_shapes=[
            pltpu.VMEM((4, 8, part), f32),
            pltpu.VMEM((chunk, part), jnp.int32),
            pltpu.VMEM((chunk, part), f32),
            pltpu.VMEM((3, cap, six * part), jnp.bfloat16),
            pltpu.VMEM((cap, part), f32),
        ],
        name="step",
    )(
        particles.reshape(six, cap, part),
        pair_order.reshape(cap, part),
        jnp.transpose(accepted.reshape(cap, pairs)),
        jnp.transpose(direction.reshape(cap, pairs)),
        destination.reshape(1, cap),
        live_count,
        cell_index.reshape(1, cap),
    )
    from_lower = from_behind(send_upper, "space", 1)
    from_upper = from_behind(send_lower, "space", -1)
    share = CELLS // reps
    my_rep = lax.axis_index("rep")
    total = lax.dynamic_slice_in_dim(cell_terms, my_rep * share, share, 1)
    for away in range(1, reps):
        theirs = lax.rem(my_rep + away, reps)
        outgoing = lax.dynamic_slice_in_dim(cell_terms, theirs * share, share, 1)
        total = total + from_behind(outgoing, "rep", away)
    samples = (total / (part * reps))[:, None, :]
    moved = lax.dynamic_update_slice(moved, from_lower, (0, 0, 0))
    moved = lax.dynamic_update_slice(moved, from_upper, (0, MOVE + cap, 0))
    return (moved[:, None], samples)


def solution(mesh):
    return jax.shard_map(
        per_device,
        mesh=mesh,
        in_specs=(
            P(None, "rep", "space", None),
            P("rep", "space", None),
            P("rep", "space", None),
            P("rep", "space", None),
            P("rep", "space"),
            P("rep", "space"),
            P("rep", "space"),
        ),
        out_specs=(P(None, "rep", "space", None), P(None, "space", "rep")),
        check_vma=False,
    )
```

time: 154 us -> 64.2 us (0.42)
  matrix products: 56 us -> 0 us
  Pallas kernels: 0 us -> 39.4 us
  local copies, waits for them, and re-layouts: 36.3 us -> 2.22 us
  other arithmetic: 26.5 us -> 1.25 us
  between operations: 14.8 us -> 1.29 us
  waiting for transfers between devices: 10.6 us -> 12.2 us
    dot_general x64 -> x0, matrix products: 55 us -> none  [the longest x32 31.5 us: collide_group(): jnp.einsum('kbp,bqp->kbq', velocity, onehot, precision=lax.Precision.HIGH...]
    pallas_call x0 -> x1, Pallas kernels: none -> 39.4 us  [per_device(): pl.pallas_call(functools.partial(main_kernel, slabs), grid=(steps,), in_s...]
    eq x32 -> x0, local copies, waits for them, and re-layouts: 22.5 us -> none  [collide_group(): onehot = (order[:, :, None] == lanes[None, None, :]).astype(jnp.float32)]
    ppermute x2 -> x3, waiting for transfers between devices: 1.44 us -> 12.2 us  [from_behind(): return lax.ppermute(value, axis, pairs)]
    select_n x37 -> x0, other arithmetic: 9.85 us -> none  [the longest x1 2.88 us: per_device(): jnp.where(keep, jnp.concatenate([position, velocity], axis=0), 0.0)]
    unnamed x2 -> x0, waiting for transfers between devices: 9.14 us -> none
    reduce_sum x36 -> x0, other arithmetic: 6.87 us -> none  [the longest x1 2.88 us: moments(): jnp.sum(velocity[0], axis=1)]
    gather x2 -> x0, local copies, waits for them, and re-layouts: 6.1 us -> none  [the longest x1 3.05 us: per_device(): jnp.take(updated, lower_ids, axis=1)]
  transfers between devices with their start and end apart: 3 -> 3, of which waited for: 2 -> 2; matrix products, arithmetic and copies ran while one was open for 8% -> 4% of each run, Pallas kernels for 0% -> 0%
where the time goes in v1:
time: 64.2 us; the launch traced here: 63.4 us
  Pallas kernels  39.4 us (61%)
  waiting for transfers between devices  12.2 us (19%)
  starting transfers between devices  7.05 us (11%)
  local copies, waits for them, and re-layouts  2.22 us (3%)
  between operations  1.29 us (2%)
  other arithmetic  1.25 us (2%)
    pallas_call x1, Pallas kernels, per_device(): pl.pallas_call(functools.partial(main_kernel, slabs), grid=(steps,), in_s...  39.4 us
    ppermute x3, waiting for transfers between devices, from_behind(): return lax.ppermute(value, axis, pairs)  12.2 us
    ppermute x3, starting transfers between devices, from_behind(): return lax.ppermute(value, axis, pairs)  7.05 us
  transfers between devices with their start and end apart: 3, of which 2 were waited for; matrix products, arithmetic and copies ran while one was open for 4% of the time, Pallas kernels for 0%

profile of v1, /device:TPU:0, one launch (start us, length us, event | category | flops | bytes accessed | tf_op | source)
XLA Modules:
  0.0 63.4 jit_solution(10745364314288197437)
XLA Ops:
  1.3 39.4 %step.1 = (f32[6,768,128]{2,1,0:T(8,128)}, f32[6,128,128]{2,1,0:T(8,128)}, f32[6,128,128]{2,1,0:T(8,128)}, f32[4,256]{1,0:T(4,128)}) custom-call(f32[6,512,128]{2,1,0:T(8,128)} %bitcast.17, s32[512,128]{1,0:T(8,128)} %bitcast.18, s32[64,512]{1,0:T(8,128)} %bitcast.19, s32[64,512]{1,0:T(8,128)} %bitcast.20, s32[1,512]{1,0:T(1,128)} %dest_ref.1, ...), custom_call_target="tpu_custom_call" | custom-call | tf_op jit(solution)/shard_map/step/pallas_call | solution.py:177
  40.6 3.0 %collective-permute-start = (f32[6,128,128]{2,1,0:T(8,128)}, f32[6,128,128]{2,1,0:T(8,128)S(1)}, u32[]{:S(2)}, u32[]{:S(2)}) collective-permute-start(f32[6,128,128]{2,1,0:T(8,128)} %get-tuple-element.7), channel_id=1, source_target_pairs={{0,1},{1,2},{2,3},{3,4},{4,5},{5,6},{6,7},{7,8},{8,9},{9,10},{10,1... | collective-permute-start | bytes 1179656 | tf_op jit(solution)/shard_map/ppermute | solution.py:165
  43.7 0.7 %constant_dynamic-slice_fusion = f32[4,128]{1,0:T(4,128)S(1)} fusion(f32[4,256]{1,0:T(4,128)} %get-tuple-element.9, s32[]{:T(128)S(6)} %select_n.7), kind=kLoop, calls=%fused_computation.3 | loop fusion | bytes 4100 | tf_op jit(solution)/shard_map/dynamic_slice | solution.py:225
  44.3 0.0 collective-permute-start.2
  44.3 4.0 %collective-permute-start.1 = (f32[6,128,128]{2,1,0:T(8,128)}, f32[6,128,128]{2,1,0:T(8,128)S(1)}, u32[]{:S(2)}, u32[]{:S(2)}) collective-permute-start(f32[6,128,128]{2,1,0:T(8,128)} %get-tuple-element.8), channel_id=1, source_target_pairs={{0,15},{1,0},{2,1},{3,2},{4,3},{5,4},{6,5},{7,6},{8,7},{9,8},{10,9... | collective-permute-start | bytes 1179656 | tf_op jit(solution)/shard_map/ppermute | solution.py:165
  48.4 0.0 collective-permute-done.2
  48.4 1.2 %add_multiply_fusion = f32[4,128]{1,0:T(4,128)} fusion(f32[4,128]{1,0:T(4,128)S(1)} %collective-permute-done.2, f32[4,256]{1,0:T(4,128)} %get-tuple-element.9, s32[]{:T(128)S(6)} %select_n.6), kind=kLoop, calls=%fused_computation.2 | loop fusion | flops 1024 | bytes 6148 | tf_op jit(solution)/shard_map/div | solution.py:227
  49.6 11.2 %collective-permute-done = f32[6,128,128]{2,1,0:T(8,128)S(1)} collective-permute-done((f32[6,128,128]{2,1,0:T(8,128)}, f32[6,128,128]{2,1,0:T(8,128)S(1)}, u32[]{:S(2)}, u32[]{:S(2)}) %collective-permute-start) | collective-permute-done | bytes 393248 | tf_op jit(solution)/shard_map/ppermute | solution.py:165
  60.8 0.8 %bitcast_dynamic-update-slice_fusion.1 = f32[6,1,768,128]{3,2,0,1:T(8,128)} fusion(f32[6,1,768,128]{3,2,0,1:T(8,128)} %bitcast.22, f32[6,128,128]{2,1,0:T(8,128)S(1)} %collective-permute-done), kind=kLoop, calls=%fused_computation.1 | loop fusion | bytes 786432 | tf_op jit(solution)/shard_map/dynamic_update_slice | solution.py:228
  61.6 1.1 %collective-permute-done.1 = f32[6,128,128]{2,1,0:T(8,128)S(1)} collective-permute-done((f32[6,128,128]{2,1,0:T(8,128)}, f32[6,128,128]{2,1,0:T(8,128)S(1)}, u32[]{:S(2)}, u32[]{:S(2)}) %collective-permute-start.1) | collective-permute-done | bytes 393248 | tf_op jit(solution)/shard_map/ppermute | solution.py:165
  62.6 0.8 %bitcast_dynamic-update-slice_fusion = f32[6,1,768,128]{3,2,0,1:T(8,128)} fusion(f32[6,1,768,128]{3,2,0,1:T(8,128)} %bitcast_dynamic-update-slice_fusion.1, f32[6,128,128]{2,1,0:T(8,128)S(1)} %collective-permute-done.1), kind=kLoop, calls=%fused_computation | loop fusion | bytes 786432 | tf_op jit(solution)/shard_map/dynamic_update_slice | solution.py:229
Async XLA Ops:
  40.6 20.1 %collective-permute-start = (f32[6,128,128]{2,1,0:T(8,128)}, f32[6,128,128]{2,1,0:T(8,128)S(1)}, u32[]{:S(2)}, u32[]{:S(2)}) collective-permute-start(f32[6,128,128]{2,1,0:T(8,128)} %get-tuple-element.7), channel_id=1, source_target_pairs={{0,1},{1,2},{2,3},{3,4},{4,5},{5,6},{6,7},{7,8},{8,9},{9,10},{10,1... | collective-permute-start | bytes 1179656 | tf_op jit(solution)/shard_map/ppermute | solution.py:165
  44.3 4.0 %collective-permute-start.2 = (f32[4,128]{1,0:T(4,128)S(1)}, f32[4,128]{1,0:T(4,128)S(1)}, u32[]{:S(2)}, u32[]{:S(2)}) collective-permute-start(f32[4,128]{1,0:T(4,128)S(1)} %constant_dynamic-slice_fusion), channel_id=1, source_target_pairs={{0,16},{16,0},{1,17},{17,1},{2,18},{18,2},{3,19},{19,3},{4,20},{20... | collective-permute-start | bytes 6152 | tf_op jit(solution)/shard_map/ppermute | solution.py:165
  44.3 18.3 %collective-permute-start.1 = (f32[6,128,128]{2,1,0:T(8,128)}, f32[6,128,128]{2,1,0:T(8,128)S(1)}, u32[]{:S(2)}, u32[]{:S(2)}) collective-permute-start(f32[6,128,128]{2,1,0:T(8,128)} %get-tuple-element.8), channel_id=1, source_target_pairs={{0,15},{1,0},{2,1},{3,2},{4,3},{5,4},{6,5},{7,6},{8,7},{9,8},{10,9... | collective-permute-start | bytes 1179656 | tf_op jit(solution)/shard_map/ppermute | solution.py:165

commit v2 on v1

v2 whole, which is shorter than its diff:
```python
import functools

import jax
import jax.numpy as jnp
from jax import lax
from jax.experimental import pallas as pl
from jax.experimental.pallas import tpu as pltpu
from jax.sharding import PartitionSpec as P


NDIR = 256
MOVE = 128
CELLS = 256
TIME_STEP = 0.25
GOLDEN_TURN = 2.399963229728653
ROWS = 128


def take_lanes(values, index):
    return jnp.take_along_axis(values, index, axis=1, mode="promise_in_bounds")


def split3(value):
    high = value.astype(jnp.bfloat16)
    rest = value - high.astype(jnp.float32)
    middle = rest.astype(jnp.bfloat16)
    low = (rest - middle.astype(jnp.float32)).astype(jnp.bfloat16)
    return high, middle, low


def dot(left, right):
    return jnp.dot(left, right, preferred_element_type=jnp.float32)


def dot_nt(left, right):
    return lax.dot_general(left, right, (((1,), (1,)), ((), ())), preferred_element_type=jnp.float32)


def inverse_order(order):
    chunk, part = order.shape
    count = part // 8
    lane = lax.broadcasted_iota(jnp.int32, (chunk, part), 1)
    keys = jnp.transpose((order * part + lane).astype(jnp.float32))
    rows = [keys[8 * i:8 * i + 8] for i in range(count)]
    sublane = lax.broadcasted_iota(jnp.int32, (8, chunk), 0)
    sign = None
    size = 2
    while size <= part:
        wanted = None
        if count <= size < part:
            wanted = jnp.where((sublane & (size // count)) == 0, 1.0, -1.0)
        if sign is not None or wanted is not None:
            flip = wanted if sign is None else sign if wanted is None else sign * wanted
            rows = [row * flip for row in rows]
        sign = wanted
        stride = size // 2
        while stride >= 1:
            if stride >= count:
                apart = stride // count
                is_low = (sublane & apart) == 0
                swapped = [jnp.take_along_axis(row, sublane ^ apart, axis=0, mode="promise_in_bounds") for row in rows]
                rows = [jnp.where(is_low, jnp.minimum(r, o), jnp.maximum(r, o)) for r, o in zip(rows, swapped)]
            else:
                after = list(rows)
                for i in range(count):
                    j = i ^ stride
                    rising = size >= count or (i & size) == 0
                    pick = jnp.minimum if (i < j) == rising else jnp.maximum
                    after[i] = pick(rows[i], rows[j])
                rows = after
            stride //= 2
        size *= 2
    ranked = [(row - ((sublane * count + i) * part).astype(jnp.float32)) for i, row in enumerate(rows)]
    placed = jnp.transpose(jnp.concatenate(ranked, axis=0)).astype(jnp.int32)
    return take_lanes(placed, (lane & (count - 1)) * 8 + lane // count)


def pick_rows(chosen, pieces):
    return dot(chosen, pieces[0]) + dot(chosen, pieces[1]) + dot(chosen, pieces[2])


def one_hot_rows(slots, cap):
    slot = lax.broadcasted_iota(jnp.int32, (MOVE, cap), 0)
    return jnp.concatenate(
        [jnp.where(slot == slots[j:j + 1, :], 1.0, 0.0) for j in range(2)], axis=0
    ).astype(jnp.bfloat16)


def first_kernel(slabs, part_ref, dest_ref, live_ref, up_ref, down_ref, slot_ref):
    cap = dest_ref.shape[1]
    chunk = MOVE
    my_slab = lax.axis_index("space")
    upper_slab = lax.rem(my_slab + 1, slabs)
    lower_slab = lax.rem(my_slab + slabs - 1, slabs)
    living = lax.broadcasted_iota(jnp.int32, (1, cap), 1) < live_ref[0, 0]
    leaving = [living & (dest_ref[...] == upper_slab), living & (dest_ref[...] == lower_slab)]
    flags = jnp.concatenate([jnp.where(m, 1.0, 0.0) for m in leaving], axis=0)
    triangle = (
        lax.broadcasted_iota(jnp.int32, (chunk, chunk), 0) <= lax.broadcasted_iota(jnp.int32, (chunk, chunk), 1)
    )
    triangle = jnp.where(triangle, 1.0, 0.0).astype(jnp.bfloat16)
    before = jnp.zeros((2, 1), jnp.float32)
    ranks = []
    for i in range(cap // chunk):
        piece = flags[:, i * chunk:(i + 1) * chunk]
        inside = dot(piece.astype(jnp.bfloat16), triangle)
        ranks.append(inside + before)
        before = before + inside[:, chunk - 1:chunk]
    ranking = jnp.concatenate(ranks, axis=1)
    slots = jnp.where(flags > 0.0, ranking - 1.0, -1.0).astype(jnp.int32)
    slot_ref[...] = slots
    chosen = one_hot_rows(slots, cap)
    for k in range(3):
        sent = pick_rows(chosen, split3(part_ref[k]))
        up_ref[k] = sent[:MOVE]
        down_ref[k] = sent[MOVE:]


def main_kernel(part_ref, order_ref, flag_ref, turn_ref, dest_ref, live_ref, cell_ref, slot_ref,
                moved_ref, up_ref, down_ref, cells_ref, table, packed_t, keep_t, inverse_t, parts, square):
    step = pl.program_id(0)
    steps = pl.num_programs(0)
    chunk, part = order_ref.shape
    pairs = part // 2
    cap = dest_ref.shape[1]
    reps, _, share = cells_ref.shape
    my_slab = lax.axis_index("space")

    @pl.when(step == 0)
    def _():
        for half in range(2):
            turns = (lax.broadcasted_iota(jnp.int32, (8, part), 1) + half * part).astype(jnp.float32)
            height = 1.0 - (2.0 * turns + 1.0) / NDIR
            radius = jnp.sqrt(1.0 - height * height)
            angle = turns * GOLDEN_TURN
            table[half] = radius * jnp.cos(angle)
            table[half + 2] = radius * jnp.sin(angle)

    pair_code = turn_ref[...] + NDIR * flag_ref[...]
    packed_t[...] = jnp.transpose(jnp.concatenate([pair_code, pair_code], axis=0))
    start = pl.multiple_of(step * chunk, chunk)
    slots = lax.broadcasted_iota(jnp.int32, (1, chunk), 1) + step * chunk
    staying = (dest_ref[:, pl.ds(start, chunk)] == my_slab) & (slots < live_ref[0, 0])
    stay_rows = jnp.broadcast_to(jnp.where(staying, 1.0, 0.0), (part, chunk))
    keep_t[...] = jnp.transpose(stay_rows)
    inverse_t[...] = inverse_order(order_ref[...])

    def rows_step(i, carry):
        row = pl.multiple_of(i * ROWS, ROWS)
        here = pl.ds(row, ROWS)
        order = order_ref[here, :]
        inverse = inverse_t[here, :]
        partner = take_lanes(order, inverse ^ pairs)
        code = take_lanes(packed_t[here, :], inverse & (pairs - 1))
        taken = code >= NDIR
        turn = code & (NDIR - 1)
        low_index = turn & (part - 1)
        is_high = turn >= part
        wide = (ROWS, part)
        tables = [jnp.broadcast_to(table[k, 0:1, :], wide) for k in range(4)]
        unit_x = jnp.where(is_high, take_lanes(tables[1], low_index), take_lanes(tables[0], low_index))
        unit_y = jnp.where(is_high, take_lanes(tables[3], low_index), take_lanes(tables[2], low_index))
        unit_z = 1.0 - (2.0 * turn.astype(jnp.float32) + 1.0) / NDIR
        old = [part_ref[3 + k, here, :] for k in range(3)]
        other = [take_lanes(v, partner) for v in old]
        relative = [a - b for a, b in zip(old, other)]
        speed = jnp.sqrt(relative[0] * relative[0] + relative[1] * relative[1] + relative[2] * relative[2])
        half_speed = jnp.where(inverse < pairs, 0.5, -0.5) * speed
        new = [
            jnp.where(taken, 0.5 * (a + b) + half_speed * u, a)
            for a, b, u in zip(old, other, (unit_x, unit_y, unit_z))
        ]
        keep = keep_t[here, :] > 0.0
        block = pl.ds(pl.multiple_of(step * chunk + row, ROWS), ROWS)
        square[block, :] = new[0] * new[0] + new[1] * new[1] + new[2] * new[2]
        for k in range(3):
            moved_ref[k, here, :] = jnp.where(keep, part_ref[k, here, :] + TIME_STEP * new[k], 0.0)
            moved_ref[3 + k, here, :] = jnp.where(keep, new[k], 0.0)
            for j, piece in enumerate(split3(new[k])):
                parts[j, block, pl.ds(k * part, part)] = piece
        return carry

    lax.fori_loop(0, chunk // ROWS, rows_step, 0)

    @pl.when(step == steps - 1)
    def _():
        chosen = one_hot_rows(slot_ref[...], cap)
        for k in range(3):
            sent = pick_rows(chosen, [parts[j, :, pl.ds(k * part, part)] for j in range(3)])
            up_ref[k] = sent[:MOVE]
            down_ref[k] = sent[MOVE:]

        living = lax.broadcasted_iota(jnp.int32, (1, cap), 1) < live_ref[0, 0]
        ones = jnp.ones((8, part), jnp.bfloat16)
        eight = lax.broadcasted_iota(jnp.int32, (8, cap), 0)
        terms = []
        for k in range(3):
            here = pl.ds(k * part, part)
            terms.append(dot_nt(ones, parts[0, :, here]) + dot_nt(ones, parts[1, :, here]) + dot_nt(ones, parts[2, :, here]))
        pieces = split3(square[...])
        terms.append(dot_nt(ones, pieces[0]) + dot_nt(ones, pieces[1]) + dot_nt(ones, pieces[2]))
        term = jnp.where(eight == 0, terms[0], jnp.where(eight == 1, terms[1], jnp.where(eight == 2, terms[2], terms[3])))
        term = jnp.where(living, term, 0.0)
        shifted = cell_ref[...] + (CELLS - lax.axis_index("rep") * share)
        shifted = jnp.where(shifted >= CELLS, shifted - CELLS, shifted)
        cells = lax.broadcasted_iota(jnp.int32, (CELLS, cap), 0)
        in_cell = jnp.where(cells == shifted, 1.0, 0.0).astype(jnp.bfloat16)
        high, middle, low = split3(term)
        total = dot_nt(high, in_cell) + dot_nt(middle, in_cell) + dot_nt(low, in_cell)
        for j in range(reps):
            cells_ref[j] = total[0:4, j * share:(j + 1) * share]


def from_behind(value, axis, steps):
    count = lax.axis_size(axis)
    pairs = [(source, (source + steps) % count) for source in range(count)]
    return lax.ppermute(value, axis, pairs)


def per_device(particles, pair_order, accepted, direction, destination, live_count, cell_index):
    six, _, cap, part = particles.shape
    three = six // 2
    pairs = accepted.shape[2]
    chunk = MOVE
    steps = cap // chunk
    slabs = lax.axis_size("space")
    reps = lax.axis_size("rep")
    share = CELLS // reps
    f32 = jnp.float32
    out_cap = cap + 2 * MOVE
    current = particles.reshape(six, cap, part)
    targets = destination.reshape(1, cap)
    parcel = jax.ShapeDtypeStruct((three, MOVE, part), f32)
    up_position, down_position, slots = pl.pallas_call(
        functools.partial(first_kernel, slabs),
        grid=(1,),
        in_specs=[
            pl.BlockSpec((three, cap, part), lambda i: (0, 0, 0)),
            pl.BlockSpec((1, cap), lambda i: (0, 0)),
            pl.BlockSpec(memory_space=pltpu.SMEM),
        ],
        out_specs=[
            pl.BlockSpec((three, MOVE, part), lambda i: (0, 0, 0)),
            pl.BlockSpec((three, MOVE, part), lambda i: (0, 0, 0)),
            pl.BlockSpec((2, cap), lambda i: (0, 0)),
        ],
        out_shape=[parcel, parcel, jax.ShapeDtypeStruct((2, cap), jnp.int32)],
        name="first",
    )(current, targets, live_count)
    lower_position = from_behind(up_position, "space", 1)
    upper_position = from_behind(down_position, "space", -1)
    collide = pl.pallas_call(
        main_kernel,
        grid=(steps,),
        in_specs=[
            pl.BlockSpec((six, chunk, part), lambda i: (0, i, 0)),
            pl.BlockSpec((chunk, part), lambda i: (i, 0)),
            pl.BlockSpec((pairs, chunk), lambda i: (0, i)),
            pl.BlockSpec((pairs, chunk), lambda i: (0, i)),
            pl.BlockSpec((1, cap), lambda i: (0, 0)),
            pl.BlockSpec(memory_space=pltpu.SMEM),
            pl.BlockSpec((1, cap), lambda i: (0, 0)),
            pl.BlockSpec((2, cap), lambda i: (0, 0)),
        ],
        out_specs=[
            pl.BlockSpec((six, chunk, part), lambda i: (0, i + 1, 0)),
            pl.BlockSpec((three, MOVE, part), lambda i: (0, 0, 0)),
            pl.BlockSpec((three, MOVE, part), lambda i: (0, 0, 0)),
            pl.BlockSpec((reps, 4, share), lambda i: (0, 0, 0)),
        ],
        out_shape=[
            jax.ShapeDtypeStruct((six, out_cap, part), f32),
            parcel,
            parcel,
            jax.ShapeDtypeStruct((reps, 4, share), f32),
        ],
        scratch_shapes=[
            pltpu.VMEM((4, 8, part), f32),
            pltpu.VMEM((chunk, part), jnp.int32),
            pltpu.VMEM((chunk, part), f32),
            pltpu.VMEM((chunk, part), jnp.int32),
            pltpu.VMEM((3, cap, three * part), jnp.bfloat16),
            pltpu.VMEM((cap, part), f32),
        ],
        cost_estimate=pl.CostEstimate(flops=10 ** 9, bytes_accessed=8 * 10 ** 6, transcendentals=0),
        name="step",
    )
    operands = (
        current,
        pair_order.reshape(cap, part),
        jnp.transpose(accepted.reshape(cap, pairs)),
        jnp.transpose(direction.reshape(cap, pairs)),
        targets,
        live_count,
        cell_index.reshape(1, cap),
        slots,
    )
    moved, up_velocity, down_velocity, cell_terms = collide(*operands)
    lower_velocity = from_behind(up_velocity, "space", 1)
    upper_velocity = from_behind(down_velocity, "space", -1)
    total = cell_terms[0]
    for away in range(1, reps):
        total = total + from_behind(cell_terms[away], "rep", away)
    samples = (total / (part * reps))[:, None, :]
    for at, position, velocity in (
        (0, lower_position, lower_velocity),
        (MOVE + cap, upper_position, upper_velocity),
    ):
        arrived = jnp.concatenate([position + TIME_STEP * velocity, velocity], axis=0)
        moved = lax.dynamic_update_slice(moved, arrived, (0, at, 0))
    return (moved[:, None], samples)


def solution(mesh):
    return jax.shard_map(
        per_device,
        mesh=mesh,
        in_specs=(
            P(None, "rep", "space", None),
            P("rep", "space", None),
            P("rep", "space", None),
            P("rep", "space", None),
            P("rep", "space"),
            P("rep", "space"),
            P("rep", "space"),
        ),
        out_specs=(P(None, "rep", "space", None), P(None, "space", "rep")),
        check_vma=False,
    )
```

time: 64.2 us -> 35.6 us (0.55)
  Pallas kernels: 39.4 us -> 10.2 us
  starting transfers between devices: 7.05 us -> 12.7 us
  waiting for transfers between devices: 12.2 us -> 7.67 us
  other arithmetic: 1.25 us -> 2.84 us
  local copies, waits for them, and re-layouts: 2.22 us -> 0.68 us
    pallas_call x1 -> x2, Pallas kernels: 39.4 us -> 10.2 us  [the longest x1 7.36 us: per_device(): moved, up_velocity, down_velocity, cell_terms = collide(*operands)]
    ppermute x3 -> x5, starting transfers between devices: 7.05 us -> 12.7 us  [from_behind(): return lax.ppermute(value, axis, pairs)]
    ppermute x3 -> x5, waiting for transfers between devices: 12.2 us -> 7.67 us  [from_behind(): return lax.ppermute(value, axis, pairs)]
    dynamic_update_slice x0 -> x2, other arithmetic: none -> 1.55 us  [per_device(): moved = lax.dynamic_update_slice(moved, arrived, (0, at, 0))]
    dynamic_update_slice x2 -> x0, local copies, waits for them, and re-layouts: 1.54 us -> none  [the longest x1 0.77 us: per_device(): moved = lax.dynamic_update_slice(moved, from_upper, (0, MOVE + cap, 0))]
    squeeze x0 -> x1, local copies, waits for them, and re-layouts: none -> 0.68 us  [per_device(): total = total + from_behind(cell_terms[away], 'rep', away)]
    dynamic_slice x1 -> x0, local copies, waits for them, and re-layouts: 0.67 us -> none  [per_device(): outgoing = lax.dynamic_slice_in_dim(cell_terms, theirs * share, share, 1)]
  transfers between devices with their start and end apart: 3 -> 5, of which waited for: 2 -> 3; matrix products, arithmetic and copies ran while one was open for 4% -> 6% of each run, Pallas kernels for 0% -> 0%
where the time goes in v2:
time: 35.6 us; the launch traced here: 35.3 us
  starting transfers between devices  12.7 us (36%)
  Pallas kernels  10.2 us (29%)
  waiting for transfers between devices  7.67 us (22%)
  other arithmetic  2.84 us (8%)
  between operations  1.3 us (4%)
  local copies, waits for them, and re-layouts  0.68 us (2%)
    ppermute x5, starting transfers between devices, from_behind(): return lax.ppermute(value, axis, pairs)  12.7 us
    ppermute x5, waiting for transfers between devices, from_behind(): return lax.ppermute(value, axis, pairs)  7.67 us
    pallas_call x1, Pallas kernels, per_device(): moved, up_velocity, down_velocity, cell_terms = collide(*operands)  7.36 us
    pallas_call x1, Pallas kernels, per_device(): pl.pallas_call(functools.partial(first_kernel, slabs), grid=(1,), in_spec...  2.81 us
    dynamic_update_slice x2, other arithmetic, per_device(): moved = lax.dynamic_update_slice(moved, arrived, (0, at, 0))  1.55 us
    div x1, other arithmetic, per_device(): samples = (total / (part * reps))[:, None, :]  1.25 us
  transfers between devices with their start and end apart: 5, of which 3 were waited for; matrix products, arithmetic and copies ran while one was open for 6% of the time, Pallas kernels for 0%

profile of v2, /device:TPU:0, one launch (start us, length us, event | category | flops | bytes accessed | tf_op | source)
XLA Modules:
  0.0 35.3 jit_solution(7270639345219319219)
XLA Ops:
  1.3 2.8 %first.1 = (f32[3,128,128]{2,1,0:T(8,128)}, f32[3,128,128]{2,1,0:T(8,128)}, s32[2,512]{1,0:T(2,128)}) custom-call(f32[6,512,128]{2,1,0:T(8,128)} %bitcast.27, s32[1,512]{1,0:T(1,128)} %dest_ref.3, s32[1,1]{1,0:T(1,128)S(6)} %copy.13.live_ref), custom_call_target="tpu_custom_call" | custom-call | tf_op jit(solution)/shard_map/first/pallas_call | solution.py:234
  4.1 0.0 copy-start.1
  4.1 0.0 copy-start
  4.1 7.4 %step.1 = (f32[6,768,128]{2,1,0:T(8,128)}, f32[3,128,128]{2,1,0:T(8,128)}, f32[3,128,128]{2,1,0:T(8,128)}, f32[2,4,128]{2,1,0:T(4,128)}) custom-call(f32[6,512,128]{2,1,0:T(8,128)} %bitcast.28, s32[512,128]{1,0:T(8,128)} %bitcast.32, s32[64,512]{1,0:T(8,128)} %bitcast.33, s32[64,512]{1,0:T(8,128)} %bitcast.34, s32[1,512]{1,0:T(1,128)} %dest_ref.3, ...), custom_call_target="tpu_custom_call" | custom-call | flops 1000000000 | bytes 8000000 | tf_op jit(solution)/shard_map/step/pallas_call | solution.py:298
  11.5 0.7 %slice_bitcast_fusion = f32[4,128]{1,0:T(4,128)S(1)} fusion(f32[2,4,128]{2,1,0:T(4,128)} %get-tuple-element.15), kind=kLoop, calls=%fused_computation.8 | loop fusion | bytes 4096 | tf_op jit(solution)/shard_map/squeeze | solution.py:303
  12.1 0.5 %collective-permute-start.4 = (f32[4,128]{1,0:T(4,128)S(1)}, f32[4,128]{1,0:T(4,128)S(1)}, u32[]{:S(2)}, u32[]{:S(2)}) collective-permute-start(f32[4,128]{1,0:T(4,128)S(1)} %slice_bitcast_fusion), channel_id=1, source_target_pairs={{0,16},{16,0},{1,17},{17,1},{2,18},{18,2},{3,19},{19,3},{4,20},{20... | collective-permute-start | bytes 6152 | tf_op jit(solution)/shard_map/ppermute | solution.py:217
  12.6 0.0 copy-done.1
  12.6 2.5 %collective-permute-start = (f32[3,128,128]{2,1,0:T(8,128)S(1)}, f32[3,128,128]{2,1,0:T(8,128)S(1)}, u32[]{:S(2)}, u32[]{:S(2)}) collective-permute-start(f32[3,128,128]{2,1,0:T(8,128)S(1)} %copy-done.1), channel_id=1, source_target_pairs={{0,1},{1,2},{2,3},{3,4},{4,5},{5,6},{6,7},{7,8},{8,9},{9,10},{10,1... | collective-permute-start | bytes 589832 | tf_op jit(solution)/shard_map/ppermute | solution.py:217
  15.1 0.0 copy-done
  15.1 4.1 %collective-permute-start.2 = (f32[3,128,128]{2,1,0:T(8,128)S(1)}, f32[3,128,128]{2,1,0:T(8,128)S(1)}, u32[]{:S(2)}, u32[]{:S(2)}) collective-permute-start(f32[3,128,128]{2,1,0:T(8,128)S(1)} %copy-done), channel_id=1, source_target_pairs={{0,15},{1,0},{2,1},{3,2},{4,3},{5,4},{6,5},{7,6},{8,7},{9,8},{10,9... | collective-permute-start | bytes 589832 | tf_op jit(solution)/shard_map/ppermute | solution.py:217
  19.2 0.0 collective-permute-start.1
  19.2 5.6 %collective-permute-start.3 = (f32[3,128,128]{2,1,0:T(8,128)}, f32[3,128,128]{2,1,0:T(8,128)S(1)}, u32[]{:S(2)}, u32[]{:S(2)}) collective-permute-start(f32[3,128,128]{2,1,0:T(8,128)} %get-tuple-element.14), channel_id=1, source_target_pairs={{0,15},{1,0},{2,1},{3,2},{4,3},{5,4},{6,5},{7,6},{8,7},{9,8},{10,9... | collective-permute-start | bytes 589832 | tf_op jit(solution)/shard_map/ppermute | solution.py:217
  24.8 0.0 collective-permute-done.4
  24.8 1.2 %fusion.2 = f32[4,128]{1,0:T(4,128)} fusion(f32[4,128]{1,0:T(4,128)S(1)} %collective-permute-done.4, f32[2,4,128]{2,1,0:T(4,128)} %get-tuple-element.15), kind=kLoop, calls=%fused_computation.7 | loop fusion | flops 1024 | bytes 6144 | tf_op jit(solution)/shard_map/div | solution.py:304
  26.0 2.8 %collective-permute-done = f32[3,128,128]{2,1,0:T(8,128)S(1)} collective-permute-done((f32[3,128,128]{2,1,0:T(8,128)S(1)}, f32[3,128,128]{2,1,0:T(8,128)S(1)}, u32[]{:S(2)}, u32[]{:S(2)}) %collective-permute-start) | collective-permute-done | bytes 196640 | tf_op jit(solution)/shard_map/ppermute | solution.py:217
  28.8 3.9 %collective-permute-done.1 = f32[3,128,128]{2,1,0:T(8,128)S(1)} collective-permute-done((f32[3,128,128]{2,1,0:T(8,128)}, f32[3,128,128]{2,1,0:T(8,128)S(1)}, u32[]{:S(2)}, u32[]{:S(2)}) %collective-permute-start.1) | collective-permute-done | bytes 196640 | tf_op jit(solution)/shard_map/ppermute | solution.py:217
  32.7 0.8 %fusion = f32[6,1,768,128]{3,2,0,1:T(8,128)} fusion(f32[6,1,768,128]{3,2,0,1:T(8,128)} %bitcast.30, f32[3,128,128]{2,1,0:T(8,128)S(1)} %collective-permute-done.1, f32[3,128,128]{2,1,0:T(8,128)S(1)} %multiply_add_fusion.1), kind=kLoop, calls=%fused_computation.1 | loop fusion | flops 98304 | bytes 786432 | tf_op jit(solution)/shard_map/dynamic_update_slice | solution.py:310
  33.5 0.0 collective-permute-done.2
  33.5 1.0 %collective-permute-done.3 = f32[3,128,128]{2,1,0:T(8,128)S(1)} collective-permute-done((f32[3,128,128]{2,1,0:T(8,128)}, f32[3,128,128]{2,1,0:T(8,128)S(1)}, u32[]{:S(2)}, u32[]{:S(2)}) %collective-permute-start.3) | collective-permute-done | bytes 196640 | tf_op jit(solution)/shard_map/ppermute | solution.py:217
  34.5 0.8 %fusion.1 = f32[6,1,768,128]{3,2,0,1:T(8,128)} fusion(f32[6,1,768,128]{3,2,0,1:T(8,128)} %fusion, f32[3,128,128]{2,1,0:T(8,128)S(1)} %collective-permute-done.3, f32[3,128,128]{2,1,0:T(8,128)S(1)} %multiply_add_fusion), kind=kLoop, calls=%fused_computation.3 | loop fusion | flops 98304 | bytes 786432 | tf_op jit(solution)/shard_map/dynamic_update_slice | solution.py:310
  (2 shorter events, 0.0 us)
Async XLA Ops:
  4.1 8.5 %copy-start.1 = (f32[3,128,128]{2,1,0:T(8,128)S(1)}, f32[3,128,128]{2,1,0:T(8,128)}, u32[]{:S(2)}) copy-start(f32[3,128,128]{2,1,0:T(8,128)} %get-tuple-element.11) | copy-start | bytes 589828
  4.1 11.0 %copy-start = (f32[3,128,128]{2,1,0:T(8,128)S(1)}, f32[3,128,128]{2,1,0:T(8,128)}, u32[]{:S(2)}) copy-start(f32[3,128,128]{2,1,0:T(8,128)} %get-tuple-element.13) | copy-start | bytes 589828
  12.1 12.7 %collective-permute-start.4 = (f32[4,128]{1,0:T(4,128)S(1)}, f32[4,128]{1,0:T(4,128)S(1)}, u32[]{:S(2)}, u32[]{:S(2)}) collective-permute-start(f32[4,128]{1,0:T(4,128)S(1)} %slice_bitcast_fusion), channel_id=1, source_target_pairs={{0,16},{16,0},{1,17},{17,1},{2,18},{18,2},{3,19},{19,3},{4,20},{20... | collective-permute-start | bytes 6152 | tf_op jit(solution)/shard_map/ppermute | solution.py:217
  12.6 16.2 %collective-permute-start = (f32[3,128,128]{2,1,0:T(8,128)S(1)}, f32[3,128,128]{2,1,0:T(8,128)S(1)}, u32[]{:S(2)}, u32[]{:S(2)}) collective-permute-start(f32[3,128,128]{2,1,0:T(8,128)S(1)} %copy-done.1), channel_id=1, source_target_pairs={{0,1},{1,2},{2,3},{3,4},{4,5},{5,6},{6,7},{7,8},{8,9},{9,10},{10,1... | collective-permute-start | bytes 589832 | tf_op jit(solution)/shard_map/ppermute | solution.py:217
  15.1 18.4 %collective-permute-start.2 = (f32[3,128,128]{2,1,0:T(8,128)S(1)}, f32[3,128,128]{2,1,0:T(8,128)S(1)}, u32[]{:S(2)}, u32[]{:S(2)}) collective-permute-start(f32[3,128,128]{2,1,0:T(8,128)S(1)} %copy-done), channel_id=1, source_target_pairs={{0,15},{1,0},{2,1},{3,2},{4,3},{5,4},{6,5},{7,6},{8,7},{9,8},{10,9... | collective-permute-start | bytes 589832 | tf_op jit(solution)/shard_map/ppermute | solution.py:217
  19.2 13.5 %collective-permute-start.1 = (f32[3,128,128]{2,1,0:T(8,128)}, f32[3,128,128]{2,1,0:T(8,128)S(1)}, u32[]{:S(2)}, u32[]{:S(2)}) collective-permute-start(f32[3,128,128]{2,1,0:T(8,128)} %get-tuple-element.12), channel_id=1, source_target_pairs={{0,1},{1,2},{2,3},{3,4},{4,5},{5,6},{6,7},{7,8},{8,9},{9,10},{10,1... | collective-permute-start | bytes 589832 | tf_op jit(solution)/shard_map/ppermute | solution.py:217
  19.2 15.3 %collective-permute-start.3 = (f32[3,128,128]{2,1,0:T(8,128)}, f32[3,128,128]{2,1,0:T(8,128)S(1)}, u32[]{:S(2)}, u32[]{:S(2)}) collective-permute-start(f32[3,128,128]{2,1,0:T(8,128)} %get-tuple-element.14), channel_id=1, source_target_pairs={{0,15},{1,0},{2,1},{3,2},{4,3},{5,4},{6,5},{7,6},{8,7},{9,8},{10,9... | collective-permute-start | bytes 589832 | tf_op jit(solution)/shard_map/ppermute | solution.py:217

commit v3 on v2

v3 whole, which is shorter than its diff:
```python
import functools

import jax
import jax.numpy as jnp
from jax import lax
from jax.experimental import pallas as pl
from jax.experimental.pallas import tpu as pltpu
from jax.sharding import PartitionSpec as P

NDIR = 256
MOVE = 128
CELLS = 256
TIME_STEP = 0.25
GOLDEN_TURN = 2.399963229728653
ROWS = 128


def take_lanes(values, index):
    return jnp.take_along_axis(values, index, axis=1, mode="promise_in_bounds")


def split3(value):
    high = value.astype(jnp.bfloat16)
    rest = value - high.astype(jnp.float32)
    middle = rest.astype(jnp.bfloat16)
    low = (rest - middle.astype(jnp.float32)).astype(jnp.bfloat16)
    return high, middle, low


def dot(left, right):
    return jnp.dot(left, right, preferred_element_type=jnp.float32)


def dot_nt(left, right):
    return lax.dot_general(left, right, (((1,), (1,)), ((), ())), preferred_element_type=jnp.float32)


def inverse_order(order):
    chunk, part = order.shape
    count = part // 8
    lane = lax.broadcasted_iota(jnp.int32, (chunk, part), 1)
    keys = jnp.transpose((order * part + lane).astype(jnp.float32))
    rows = [keys[8 * i:8 * i + 8] for i in range(count)]
    sublane = lax.broadcasted_iota(jnp.int32, (8, chunk), 0)
    sign = None
    size = 2
    while size <= part:
        wanted = None
        if count <= size < part:
            wanted = jnp.where((sublane & (size // count)) == 0, 1.0, -1.0)
        if sign is not None or wanted is not None:
            flip = wanted if sign is None else sign if wanted is None else sign * wanted
            rows = [row * flip for row in rows]
        sign = wanted
        stride = size // 2
        while stride >= 1:
            if stride >= count:
                apart = stride // count
                is_low = (sublane & apart) == 0
                swapped = [jnp.take_along_axis(row, sublane ^ apart, axis=0, mode="promise_in_bounds") for row in rows]
                rows = [jnp.where(is_low, jnp.minimum(r, o), jnp.maximum(r, o)) for r, o in zip(rows, swapped)]
            else:
                after = list(rows)
                for i in range(count):
                    j = i ^ stride
                    rising = size >= count or (i & size) == 0
                    pick = jnp.minimum if (i < j) == rising else jnp.maximum
                    after[i] = pick(rows[i], rows[j])
                rows = after
            stride //= 2
        size *= 2
    ranked = [(row - ((sublane * count + i) * part).astype(jnp.float32)) for i, row in enumerate(rows)]
    placed = jnp.transpose(jnp.concatenate(ranked, axis=0)).astype(jnp.int32)
    return take_lanes(placed, (lane & (count - 1)) * 8 + lane // count)


def pick_rows(chosen, pieces):
    return dot(chosen, pieces[0]) + dot(chosen, pieces[1]) + dot(chosen, pieces[2])


def one_hot_rows(slots, cap):
    slot = lax.broadcasted_iota(jnp.int32, (MOVE, cap), 0)
    return jnp.concatenate(
        [jnp.where(slot == slots[j:j + 1, :], 1.0, 0.0) for j in range(2)], axis=0
    ).astype(jnp.bfloat16)


def mover_slots(dest, living, upper_slab, lower_slab):
    cap = dest.shape[1]
    chunk = MOVE
    leaving = [living & (dest == upper_slab), living & (dest == lower_slab)]
    flags = jnp.concatenate([jnp.where(m, 1.0, 0.0) for m in leaving], axis=0)
    triangle = (
        lax.broadcasted_iota(jnp.int32, (chunk, chunk), 0) <= lax.broadcasted_iota(jnp.int32, (chunk, chunk), 1)
    )
    triangle = jnp.where(triangle, 1.0, 0.0).astype(jnp.bfloat16)
    before = jnp.zeros((2, 1), jnp.float32)
    ranks = []
    for i in range(cap // chunk):
        piece = flags[:, i * chunk:(i + 1) * chunk]
        inside = dot(piece.astype(jnp.bfloat16), triangle)
        ranks.append(inside + before)
        before = before + inside[:, chunk - 1:chunk]
    ranking = jnp.concatenate(ranks, axis=1)
    return jnp.where(flags > 0.0, ranking - 1.0, -1.0).astype(jnp.int32)


def main_kernel(slabs, steps, part_ref, order_ref, flag_ref, turn_ref, dest_ref, live_ref, cell_ref, place_ref,
                moved_ref, samples_ref, table, packed_t, keep_t, inverse_t, parts, square, slot_ref,
                sent_place, sent_speed, got_place, got_speed, sent_cells, got_cells, send_sem, recv_sem):
    step = pl.program_id(0)
    chunk, part = order_ref.shape
    pairs = part // 2
    cap = dest_ref.shape[1]
    reps, _, share = sent_cells.shape
    my_slab = lax.axis_index("space")
    my_rep = lax.axis_index("rep")
    upper_slab = lax.rem(my_slab + 1, slabs)
    lower_slab = lax.rem(my_slab + slabs - 1, slabs)
    goals = (upper_slab, lower_slab)

    def copy(source, target, k, device):
        return pltpu.make_async_remote_copy(
            src_ref=source, dst_ref=target, send_sem=send_sem.at[k], recv_sem=recv_sem.at[k],
            device_id=device, device_id_type=pl.DeviceIdType.MESH,
        )

    place_copies, speed_copies = [
        [[copy(sent.at[j, k], got.at[j, k], base + 3 * j + k, {"space": goals[j]}) for k in range(3)] for j in range(2)]
        for sent, got, base in ((sent_place, got_place, 0), (sent_speed, got_speed, 6))
    ]
    cell_copies = [
        copy(sent_cells.at[k], got_cells.at[k], 11 + k, {"rep": lax.rem(my_rep + k, reps)}) for k in range(1, reps)
    ]

    @pl.when(step == 0)
    def _():
        barrier = pltpu.get_barrier_semaphore()
        for j in range(2):
            pl.semaphore_signal(barrier, inc=1, device_id={"space": goals[j]}, device_id_type=pl.DeviceIdType.MESH)
        for k in range(1, reps):
            pl.semaphore_signal(
                barrier, inc=1, device_id={"rep": lax.rem(my_rep + k, reps)}, device_id_type=pl.DeviceIdType.MESH
            )
        living = lax.broadcasted_iota(jnp.int32, (1, cap), 1) < live_ref[...]
        slots = mover_slots(dest_ref[...], living, upper_slab, lower_slab)
        slot_ref[...] = slots
        chosen = one_hot_rows(slots, cap)
        for k in range(3):
            sent = pick_rows(chosen, split3(place_ref[k]))
            sent_place[0, k] = sent[:MOVE]
            sent_place[1, k] = sent[MOVE:]
            if k == 0:
                pl.semaphore_wait(barrier, 1 + reps)
            for j in range(2):
                place_copies[j][k].start()

    @pl.when(step == 0)
    def _():
        for half in range(2):
            turns = (lax.broadcasted_iota(jnp.int32, (8, part), 1) + half * part).astype(jnp.float32)
            height = 1.0 - (2.0 * turns + 1.0) / NDIR
            radius = jnp.sqrt(1.0 - height * height)
            angle = turns * GOLDEN_TURN
            table[half] = radius * jnp.cos(angle)
            table[half + 2] = radius * jnp.sin(angle)

    @pl.when(step < steps)
    def _():
        pair_code = turn_ref[...] + NDIR * flag_ref[...]
        packed_t[...] = jnp.transpose(jnp.concatenate([pair_code, pair_code], axis=0))
        start = pl.multiple_of(step * chunk, chunk)
        slots = lax.broadcasted_iota(jnp.int32, (1, chunk), 1) + step * chunk
        staying = (dest_ref[:, pl.ds(start, chunk)] == my_slab) & (slots < live_ref[...])
        stay_rows = jnp.broadcast_to(jnp.where(staying, 1.0, 0.0), (part, chunk))
        keep_t[...] = jnp.transpose(stay_rows)
        inverse_t[...] = inverse_order(order_ref[...])

        def rows_step(i, carry):
            row = pl.multiple_of(i * ROWS, ROWS)
            here = pl.ds(row, ROWS)
            order = order_ref[here, :]
            inverse = inverse_t[here, :]
            partner = take_lanes(order, inverse ^ pairs)
            code = take_lanes(packed_t[here, :], inverse & (pairs - 1))
            taken = code >= NDIR
            turn = code & (NDIR - 1)
            low_index = turn & (part - 1)
            is_high = turn >= part
            wide = (ROWS, part)
            tables = [jnp.broadcast_to(table[k, 0:1, :], wide) for k in range(4)]
            unit_x = jnp.where(is_high, take_lanes(tables[1], low_index), take_lanes(tables[0], low_index))
            unit_y = jnp.where(is_high, take_lanes(tables[3], low_index), take_lanes(tables[2], low_index))
            unit_z = 1.0 - (2.0 * turn.astype(jnp.float32) + 1.0) / NDIR
            old = [part_ref[3 + k, here, :] for k in range(3)]
            other = [take_lanes(v, partner) for v in old]
            relative = [a - b for a, b in zip(old, other)]
            speed = jnp.sqrt(relative[0] * relative[0] + relative[1] * relative[1] + relative[2] * relative[2])
            half_speed = jnp.where(inverse < pairs, 0.5, -0.5) * speed
            new = [
                jnp.where(taken, 0.5 * (a + b) + half_speed * u, a)
                for a, b, u in zip(old, other, (unit_x, unit_y, unit_z))
            ]
            keep = keep_t[here, :] > 0.0
            target = pl.ds(pl.multiple_of(MOVE + step * chunk + row, ROWS), ROWS)
            block = pl.ds(pl.multiple_of(step * chunk + row, ROWS), ROWS)
            square[block, :] = new[0] * new[0] + new[1] * new[1] + new[2] * new[2]
            for k in range(3):
                moved_ref[k, target, :] = jnp.where(keep, part_ref[k, here, :] + TIME_STEP * new[k], 0.0)
                moved_ref[3 + k, target, :] = jnp.where(keep, new[k], 0.0)
                for j, piece in enumerate(split3(new[k])):
                    parts[j, block, pl.ds(k * part, part)] = piece
            return carry

        lax.fori_loop(0, chunk // ROWS, rows_step, 0)

    @pl.when(step == steps - 1)
    def _():
        chosen = one_hot_rows(slot_ref[...], cap)
        for k in range(3):
            sent = pick_rows(chosen, [parts[j, :, pl.ds(k * part, part)] for j in range(3)])
            sent_speed[0, k] = sent[:MOVE]
            sent_speed[1, k] = sent[MOVE:]
            for j in range(2):
                speed_copies[j][k].start()

        living = lax.broadcasted_iota(jnp.int32, (1, cap), 1) < live_ref[...]
        ones = jnp.ones((8, part), jnp.bfloat16)
        eight = lax.broadcasted_iota(jnp.int32, (8, cap), 0)
        terms = []
        for k in range(3):
            here = pl.ds(k * part, part)
            terms.append(dot_nt(ones, parts[0, :, here]) + dot_nt(ones, parts[1, :, here]) + dot_nt(ones, parts[2, :, here]))
        pieces = split3(square[...])
        terms.append(dot_nt(ones, pieces[0]) + dot_nt(ones, pieces[1]) + dot_nt(ones, pieces[2]))
        term = jnp.where(eight == 0, terms[0], jnp.where(eight == 1, terms[1], jnp.where(eight == 2, terms[2], terms[3])))
        term = jnp.where(living, term, 0.0)
        shifted = cell_ref[...] + (CELLS - my_rep * share)
        shifted = jnp.where(shifted >= CELLS, shifted - CELLS, shifted)
        cells = lax.broadcasted_iota(jnp.int32, (CELLS, cap), 0)
        in_cell = jnp.where(cells == shifted, 1.0, 0.0).astype(jnp.bfloat16)
        high, middle, low = split3(term)
        total = dot_nt(high, in_cell) + dot_nt(middle, in_cell) + dot_nt(low, in_cell)
        for j in range(reps):
            sent_cells[j] = total[0:4, j * share:(j + 1) * share]
        for each in cell_copies:
            each.start()

        total = sent_cells[0]
        for k in range(1, reps):
            cell_copies[k - 1].wait()
            total = total + got_cells[k]
        samples_ref[...] = total / (part * reps)
        for k in range(3):
            for j, at in ((0, 0), (1, MOVE + cap)):
                target = pl.ds(at, MOVE)
                place_copies[j][k].wait()
                speed_copies[j][k].wait()
                moved_ref[k, target, :] = got_place[j, k] + TIME_STEP * got_speed[j, k]
                moved_ref[3 + k, target, :] = got_speed[j, k]


def per_device(particles, pair_order, accepted, direction, destination, live_count, cell_index):
    six, _, cap, part = particles.shape
    three = six // 2
    pairs = accepted.shape[2]
    chunk = MOVE
    steps = cap // chunk
    slabs = lax.axis_size("space")
    reps = lax.axis_size("rep")
    share = CELLS // reps
    f32 = jnp.float32
    out_cap = cap + 2 * MOVE
    current = particles.reshape(six, cap, part)
    call = pl.pallas_call(
        functools.partial(main_kernel, slabs, steps),
        grid=(steps,),
        in_specs=[
            pl.BlockSpec((six, chunk, part), lambda i: (0, i, 0)),
            pl.BlockSpec((chunk, part), lambda i: (i, 0)),
            pl.BlockSpec((pairs, chunk), lambda i: (0, i)),
            pl.BlockSpec((pairs, chunk), lambda i: (0, i)),
            pl.BlockSpec((1, cap), lambda i: (0, 0)),
            pl.BlockSpec((1, 1), lambda i: (0, 0)),
            pl.BlockSpec((1, cap), lambda i: (0, 0)),
            pl.BlockSpec((three, cap, part), lambda i: (0, 0, 0)),
        ],
        out_specs=[
            pl.BlockSpec(memory_space=pltpu.VMEM),
            pl.BlockSpec((4, share), lambda i: (0, 0)),
        ],
        out_shape=[
            jax.ShapeDtypeStruct((six, out_cap, part), f32),
            jax.ShapeDtypeStruct((4, share), f32),
        ],
        scratch_shapes=[
            pltpu.VMEM((4, 8, part), f32),
            pltpu.VMEM((chunk, part), jnp.int32),
            pltpu.VMEM((chunk, part), f32),
            pltpu.VMEM((chunk, part), jnp.int32),
            pltpu.VMEM((3, cap, three * part), jnp.bfloat16),
            pltpu.VMEM((cap, part), f32),
            pltpu.VMEM((2, cap), jnp.int32),
            pltpu.VMEM((2, three, MOVE, part), f32),
            pltpu.VMEM((2, three, MOVE, part), f32),
            pltpu.VMEM((2, three, MOVE, part), f32),
            pltpu.VMEM((2, three, MOVE, part), f32),
            pltpu.VMEM((reps, 4, share), f32),
            pltpu.VMEM((reps, 4, share), f32),
            pltpu.SemaphoreType.DMA((11 + reps,)),
            pltpu.SemaphoreType.DMA((11 + reps,)),
        ],
        compiler_params=pltpu.CompilerParams(collective_id=0, has_side_effects=True, vmem_limit_bytes=16 * 2 ** 20),
        name="step",
    )
    operands = (
        current,
        pair_order.reshape(cap, part),
        jnp.transpose(accepted.reshape(cap, pairs)),
        jnp.transpose(direction.reshape(cap, pairs)),
        destination.reshape(1, cap),
        live_count,
        cell_index.reshape(1, cap),
        current,
    )
    hold = functools.partial(pltpu.with_memory_space_constraint, memory_space=pltpu.HBM)
    operands = [x if x is live_count else hold(x) for x in operands]
    moved, samples = call(*operands)
    return (moved[:, None], samples[:, None, :])


def solution(mesh):
    return jax.shard_map(
        per_device,
        mesh=mesh,
        in_specs=(
            P(None, "rep", "space", None),
            P("rep", "space", None),
            P("rep", "space", None),
            P("rep", "space", None),
            P("rep", "space"),
            P("rep", "space"),
            P("rep", "space"),
        ),
        out_specs=(P(None, "rep", "space", None), P(None, "space", "rep")),
        check_vma=False,
    )
```

time: 35.6 us -> 26.9 us (0.76)
  Pallas kernels: 10.2 us -> 23.4 us
  starting transfers between devices: 12.7 us -> 0 us
  waiting for transfers between devices: 7.67 us -> 0 us
  other arithmetic: 2.84 us -> 0 us
  local copies, waits for them, and re-layouts: 0.68 us -> 1.99 us
    pallas_call x2 -> x1, Pallas kernels: 10.2 us -> 23.4 us  [per_device(): moved, samples = call(*operands)]
    ppermute x5 -> x0, starting transfers between devices: 12.7 us -> none  [from_behind(): return lax.ppermute(value, axis, pairs)]
    ppermute x5 -> x0, waiting for transfers between devices: 7.67 us -> none  [from_behind(): return lax.ppermute(value, axis, pairs)]
    unnamed x4 -> x2, local copies, waits for them, and re-layouts: 0.01 us -> 1.99 us
    dynamic_update_slice x2 -> x0, other arithmetic: 1.55 us -> none  [per_device(): moved = lax.dynamic_update_slice(moved, arrived, (0, at, 0))]
    div x1 -> x0, other arithmetic: 1.25 us -> none  [per_device(): samples = (total / (part * reps))[:, None, :]]
    squeeze x1 -> x0, local copies, waits for them, and re-layouts: 0.68 us -> none  [per_device(): total = total + from_behind(cell_terms[away], 'rep', away)]
  transfers between devices with their start and end apart: 5 -> 0, of which waited for: 3 -> 0; matrix products, arithmetic and copies ran while one was open for 6% -> 0% of each run, Pallas kernels for 0% -> 0%
where the time goes in v3:
time: 26.9 us; the launch traced here: 26.7 us
  Pallas kernels  23.4 us (87%)
  local copies, waits for them, and re-layouts  1.99 us (7%)
  between operations  1.29 us (5%)
    pallas_call x1, Pallas kernels, per_device(): moved, samples = call(*operands)  23.4 us
    unnamed x2, local copies, waits for them, and re-layouts  1.99 us

profile of v3, /device:TPU:0, one launch (start us, length us, event | category | flops | bytes accessed | tf_op | source)
XLA Modules:
  0.0 26.7 jit_solution(18139167749214956153)
XLA Ops:
  1.3 23.4 %step.1 = (f32[6,768,128]{2,1,0:T(8,128)S(1)}, f32[4,128]{1,0:T(4,128)S(1)}) custom-call(f32[6,512,128]{2,1,0:T(8,128)} %bitcast.16, s32[512,128]{1,0:T(8,128)} %bitcast.18, s32[64,512]{1,0:T(8,128)} %bitcast.19, s32[64,512]{1,0:T(8,128)} %bitcast.20, s32[1,512]{1,0:T(1,128)} %dest_ref.1, s32[1,1]{1,0:T(1,128)S(6)} %copy.13.live_ref, s32[1,512]{1,0:T(1,128)} %cell_ref.1, ...), custom_call_target="tpu_custom_call" | custom-call | tf_op jit(solution)/shard_map/step/pallas_call | solution.py:328
  24.7 1.4 %copy.14 = f32[6,1,768,128]{3,2,1,0:T(8,128)} copy(f32[6,1,768,128]{3,2,1,0:T(8,128)S(1)} %bitcast.14) | data formatting | bytes 4718592
  26.1 0.6 %copy.15 = f32[4,1,128]{2,1,0:T(1,128)} copy(f32[4,1,128]{2,1,0:T(1,128)S(1)} %bitcast.15) | data formatting | bytes 4096

commit v4 on v3

--- a/solution.py
+++ b/solution.py
@@ -107,7 +107,7 @@
 
 def main_kernel(slabs, steps, part_ref, order_ref, flag_ref, turn_ref, dest_ref, live_ref, cell_ref, place_ref,
                 moved_ref, samples_ref, table, packed_t, keep_t, inverse_t, parts, square, slot_ref,
-                sent_place, sent_speed, got_place, got_speed, sent_cells, got_cells, send_sem, recv_sem):
+                sent_place, sent_speed, got_place, got_speed, sent_cells, got_cells, send_sem, recv_sem, places, load_sem):
     step = pl.program_id(0)
     chunk, part = order_ref.shape
     pairs = part // 2
@@ -142,12 +142,15 @@
             pl.semaphore_signal(
                 barrier, inc=1, device_id={"rep": lax.rem(my_rep + k, reps)}, device_id_type=pl.DeviceIdType.MESH
             )
+        load = pltpu.make_async_copy(place_ref.at[pl.ds(0, 3)], places, load_sem)
+        load.start()
         living = lax.broadcasted_iota(jnp.int32, (1, cap), 1) < live_ref[...]
         slots = mover_slots(dest_ref[...], living, upper_slab, lower_slab)
         slot_ref[...] = slots
         chosen = one_hot_rows(slots, cap)
+        load.wait()
         for k in range(3):
-            sent = pick_rows(chosen, split3(place_ref[k]))
+            sent = pick_rows(chosen, split3(places[k]))
             sent_place[0, k] = sent[:MOVE]
             sent_place[1, k] = sent[MOVE:]
             if k == 0:
@@ -250,7 +253,9 @@
         for k in range(1, reps):
             cell_copies[k - 1].wait()
             total = total + got_cells[k]
-        samples_ref[...] = total / (part * reps)
+        total = total / (part * reps)
+        for k in range(4):
+            samples_ref[k] = total[k:k + 1]
         for k in range(3):
             for j, at in ((0, 0), (1, MOVE + cap)):
                 target = pl.ds(at, MOVE)
@@ -283,15 +288,15 @@
             pl.BlockSpec((1, cap), lambda i: (0, 0)),
             pl.BlockSpec((1, 1), lambda i: (0, 0)),
             pl.BlockSpec((1, cap), lambda i: (0, 0)),
-            pl.BlockSpec((three, cap, part), lambda i: (0, 0, 0)),
+            pl.BlockSpec(memory_space=pltpu.HBM),
         ],
         out_specs=[
             pl.BlockSpec(memory_space=pltpu.VMEM),
-            pl.BlockSpec((4, share), lambda i: (0, 0)),
+            pl.BlockSpec((4, 1, share), lambda i: (0, 0, 0)),
         ],
         out_shape=[
             jax.ShapeDtypeStruct((six, out_cap, part), f32),
-            jax.ShapeDtypeStruct((4, share), f32),
+            jax.ShapeDtypeStruct((4, 1, share), f32),
         ],
         scratch_shapes=[
             pltpu.VMEM((4, 8, part), f32),
@@ -309,6 +314,8 @@
             pltpu.VMEM((reps, 4, share), f32),
             pltpu.SemaphoreType.DMA((11 + reps,)),
             pltpu.SemaphoreType.DMA((11 + reps,)),
+            pltpu.VMEM((three, cap, part), f32),
+            pltpu.SemaphoreType.DMA,
         ],
         compiler_params=pltpu.CompilerParams(collective_id=0, has_side_effects=True, vmem_limit_bytes=16 * 2 ** 20),
         name="step",
@@ -326,7 +333,7 @@
     hold = functools.partial(pltpu.with_memory_space_constraint, memory_space=pltpu.HBM)
     operands = [x if x is live_count else hold(x) for x in operands]
     moved, samples = call(*operands)
-    return (moved[:, None], samples[:, None, :])
+    return (moved[:, None], samples)
 
 
 def solution(mesh):

time: 26.9 us -> 26.9 us (level)
  no operation moved by 1% of the time
where the time goes in v4:
time: 26.9 us; the launch traced here: 26.7 us
  Pallas kernels  23.4 us (87%)
  local copies, waits for them, and re-layouts  1.99 us (7%)
  between operations  1.29 us (5%)
    pallas_call x1, Pallas kernels, per_device(): moved, samples = call(*operands)  23.4 us
    unnamed x2, local copies, waits for them, and re-layouts  1.99 us

profile of v4, /device:TPU:0, one launch (start us, length us, event | category | flops | bytes accessed | tf_op | source)
XLA Modules:
  0.0 26.7 jit_solution(16658297207239990389)
XLA Ops:
  1.3 23.4 %step.1 = (f32[6,768,128]{2,1,0:T(8,128)S(1)}, f32[4,1,128]{2,1,0:T(1,128)S(1)}) custom-call(f32[6,512,128]{2,1,0:T(8,128)} %bitcast.12, s32[512,128]{1,0:T(8,128)} %bitcast.14, s32[64,512]{1,0:T(8,128)} %bitcast.15, s32[64,512]{1,0:T(8,128)} %bitcast.16, s32[1,512]{1,0:T(1,128)} %dest_ref.1, s32[1,1]{1,0:T(1,128)S(6)} %copy.12.live_ref, s32[1,512]{1,0:T(1,128)} %cell_ref.1, ...), custom_call_target="tpu_custom_call" | custom-call | tf_op jit(solution)/shard_map/step/pallas_call | solution.py:335
  24.7 1.4 %copy.13 = f32[6,1,768,128]{3,2,1,0:T(8,128)} copy(f32[6,1,768,128]{3,2,1,0:T(8,128)S(1)} %bitcast.11) | data formatting | bytes 4718592
  26.1 0.6 %copy.14 = f32[4,1,128]{2,1,0:T(1,128)} copy(f32[4,1,128]{2,1,0:T(1,128)S(1)} %get-tuple-element.11) | data formatting | bytes 4096
